TPU v7x, 32 devices: a whole 2x2x4 slice. The times are simulated.
32 devices in a mesh: lat: 8 (over z, x), fld: 4 (over y, core).
Axes of the slice: x: 2, y: 2, z: 4, core: 2. Of those that a mesh axis runs over, the one named last changes fastest.
Arguments:
- field_grid: bfloat16 [8, 2560, 5120], P('fld', 'lat'), may hold values from -300 to 300
- wave_table: int32 [64], replicated, may hold values from 0 to 1279, as said below
- legendre: bfloat16 [64, 2, 640, 1280], P('lat', None, 'fld'), may hold values from -0.15625 to 0.15625
Outputs:
- spectral: float32 [64, 640, 32], P('lat', 'fld')
Inputs may be any that keep to these rules, and one draw needn't show every extreme that they name: `wave_table`: the entries differ from one another; each aligned block of 8 entries owned by one index of lat is made of pairs m and 1279 - m, next to each other.
All inputs are finite; a program needn't handle non-finite values.
Results may differ from a plain program's by a relative error of at most 0.0048.
Values may be sent and summed in bfloat16 or wider, within the bound.
A program may use at most 64 MiB of HBM per device.

v0:
```python
import functools
import math

import jax
import jax.numpy as jnp
from jax import lax
from jax.experimental import pallas as pl
from jax.experimental.pallas import tpu as pltpu
from jax.sharding import PartitionSpec as P

TWO_PI = 2.0 * math.pi


def twiddle_block(wave_block, lon_total):
    fine_count = math.gcd(lon_total, 128)
    coarse_count = lon_total // fine_count
    waves = wave_block[:, None]
    coarse_index = (
        waves * (jnp.arange(coarse_count, dtype=jnp.int32) * fine_count)[None, :] % lon_total
    )
    fine_index = waves * jnp.arange(fine_count, dtype=jnp.int32)[None, :] % lon_total
    coarse_angle = coarse_index.astype(jnp.float32) * (TWO_PI / lon_total)
    fine_angle = fine_index.astype(jnp.float32) * (TWO_PI / lon_total)
    coarse_cos = jnp.cos(coarse_angle)[:, :, None]
    coarse_sin = jnp.sin(coarse_angle)[:, :, None]
    fine_cos = jnp.cos(fine_angle)[:, None, :]
    fine_sin = jnp.sin(fine_angle)[:, None, :]
    cosine = (coarse_cos * fine_cos - coarse_sin * fine_sin).reshape(wave_block.shape[0], lon_total)
    minus_sine = (-(coarse_sin * fine_cos + coarse_cos * fine_sin)).reshape(
        wave_block.shape[0], lon_total
    )
    return jnp.concatenate([cosine, minus_sine], axis=0).astype(jnp.bfloat16)


def fold_halves(fourier):
    half_lat = fourier.shape[-1] // 2
    north_rows = fourier[..., :half_lat].astype(jnp.float32)
    south_rows = jnp.flip(fourier[..., half_lat:], axis=-1).astype(jnp.float32)
    return jnp.stack([north_rows + south_rows, north_rows - south_rows], axis=1).astype(
        jnp.bfloat16
    )


def shards_by_collectives(field_grid, wave_table, legendre):
    f_dev, lat_dev, lon_total = field_grid.shape
    slot_total = wave_table.shape[0]
    slot_dev = legendre.shape[0]
    row_dev = legendre.shape[2]
    grid_rows = field_grid.reshape(f_dev * lat_dev, lon_total)
    block_size = math.gcd(slot_total, 256)
    wave_blocks = wave_table.reshape(slot_total // block_size, block_size)

    def transform(wave_block):
        twiddle = twiddle_block(wave_block, lon_total)
        spectra = lax.dot_general(
            twiddle, grid_rows, (((1,), (1,)), ((), ())), preferred_element_type=jnp.float32
        )
        spectra = (spectra * (1.0 / lon_total)).astype(jnp.bfloat16)
        return jnp.transpose(spectra.reshape(2, block_size, f_dev, lat_dev), (1, 0, 2, 3))

    fourier = lax.map(transform, wave_blocks).reshape(slot_total, 2, f_dev, lat_dev)
    first_slot = lax.axis_index("lat") * slot_dev
    own_waves = lax.dynamic_slice_in_dim(wave_table, first_slot, slot_dev)
    trunc_total = 2 * row_dev * lax.axis_size("fld")
    row_index = lax.axis_index("fld") * row_dev + jnp.arange(row_dev, dtype=jnp.int32)
    parity = jnp.arange(2, dtype=jnp.int32)
    degree = own_waves[:, None, None] + 2 * row_index[None, :, None] + parity[None, None, :]
    valid_mask = (degree <= trunc_total - 1).astype(jnp.float32)
    regrouped = lax.all_to_all(fourier, "lat", split_axis=0, concat_axis=3, tiled=True)
    folded = fold_halves(regrouped)
    folded_piece = lax.all_gather(folded, "fld", axis=3, tiled=True)
    parts_count = folded_piece.shape[2]
    width = folded_piece.shape[3]
    merged = folded_piece.reshape(slot_dev, 2, parts_count * width, folded_piece.shape[4])
    coeffs = jnp.einsum("sprj,spcj->srpc", legendre, merged, preferred_element_type=jnp.float32)
    coeffs = coeffs.reshape(slot_dev, row_dev, 2, parts_count, width)
    coeffs = coeffs * valid_mask[:, :, :, None, None]
    return coeffs.reshape(slot_dev, row_dev, -1)


LANES = 128
HALF = 64
MESH = pl.DeviceIdType.MESH


def sin_cos_of_phase(phase, period):
    turns = jnp.floor(phase * (1.0 / period))
    rest = phase - turns * period
    rest = jnp.where(rest < 0, rest + period, rest)
    rest = jnp.where(rest >= period, rest - period, rest)
    eighth = period / 8
    q0 = rest < eighth
    q1 = rest < 3 * eighth
    q2 = rest < 5 * eighth
    q3 = rest < 7 * eighth
    centre = jnp.where(
        q0, 0.0, jnp.where(q1, 2 * eighth, jnp.where(q2, 4 * eighth, jnp.where(q3, 6 * eighth, period)))
    )
    x = (rest - centre) * (TWO_PI / period)
    y = x * x
    s = x * (1.0 + y * (-1 / 6 + y * (1 / 120 + y * (-1 / 5040 + y * (1 / 362880)))))
    c = 1.0 + y * (-1 / 2 + y * (1 / 24 + y * (-1 / 720 + y * (1 / 40320 - y * (1 / 3628800)))))
    even = q0 | (q2 & ~q1) | ~q3
    minus_sin = (q3 & ~q1)
    minus_cos = (q2 & ~q0)
    sine = jnp.where(even, s, c)
    sine = jnp.where(minus_sin, -sine, sine)
    cosine = jnp.where(even, c, s)
    cosine = jnp.where(minus_cos, -cosine, cosine)
    return sine, cosine


def transform_kernel(
    lat_count, wave_hbm, wave_row_hbm, field_ref, legendre_ref, out_ref,
    grid, twiddle, coarse, table, send, recv, folded, partial, spun, wave_smem, wave_row,
    field_sem, wave_sem, table_sem, sent, lat_recv, y_recv, c_recv, d_recv,
):
    lat = lax.axis_index("lat")
    fld = lax.axis_index("fld")
    y_peer = (fld + 2) % 4
    partner = fld + 1 - 2 * (fld % 2)
    partner_y = (partner + 2) % 4

    _, lat_dev, lon_total = field_ref.shape
    main = lat_dev // LANES
    tiles = 2 * main + 1
    slot_dev, _, row_dev, _ = legendre_ref.shape
    slot_total = wave_row_hbm.shape[1]
    half_lats = lat_count // 2
    chunk_tiles = ((0, 1), (1, main + 1), (main + 1, tiles))
    chunk_count = len(chunk_tiles)

    def band_of(index):
        south = index // half_lats
        return south, index + south * (lat_count - 1 - 2 * index)

    def place_of(index):
        south, band = band_of(index)
        return 2 * band + south

    south, band = band_of(lat)
    place = place_of(lat)
    odd = band % 2
    mixed = (south + odd) % 2

    def chunk_of(t):
        return [low <= t < high for low, high in chunk_tiles].index(True)

    def load(f, row, count, dst):
        pltpu.make_async_copy(
            field_ref.at[f, pl.ds(pl.multiple_of(row, HALF), count)],
            grid.at[pl.ds(pl.multiple_of(dst, HALF), count)],
            field_sem.at[chunk_of(load_tile[0])],
        ).start(priority=1)

    load_tile = [0]

    def load_main(f, t, dst_tile):
        load_tile[0] = dst_tile
        north_row = LANES * t + HALF * odd
        south_row = lat_dev - LANES - LANES * t - HALF * odd
        load(f, north_row + south * (south_row - north_row), LANES, LANES * dst_tile)

    wave_copies = [
        pltpu.make_async_copy(wave_row_hbm, wave_row, wave_sem.at[0]),
        pltpu.make_async_copy(wave_hbm, wave_smem, wave_sem.at[1]),
    ]
    for copy in wave_copies:
        copy.start()
    for t in range(main):
        load_main(0, t, t)
    load_tile[0] = main
    tail_row = (lat_dev - HALF) * (1 - mixed)
    load(0, tail_row, HALF, LANES * main + HALF * mixed)
    load(1, tail_row, HALF, LANES * main + HALF * (1 - mixed))
    for t in range(main):
        load_main(1, t, main + 1 + t)

    barrier = pltpu.get_barrier_semaphore()
    for d in range(1, lat_count):
        pl.semaphore_signal(
            barrier, inc=1, device_id=((lat + d) % lat_count, fld), device_id_type=MESH
        )
    for other in (y_peer, partner):
        pl.semaphore_signal(barrier, inc=1, device_id=(lat, other), device_id_type=MESH)

    for copy in wave_copies:
        copy.wait()
    waves = wave_row[...].astype(jnp.float32)
    waves = jnp.concatenate([waves, waves], axis=1)
    width = 2 * slot_total
    coarse_count = lon_total // LANES
    k_fine = lax.broadcasted_iota(jnp.int32, (LANES, width), 0).astype(jnp.float32)
    is_sine = lax.broadcasted_iota(jnp.int32, (LANES, width), 1) >= slot_total
    quarter = jnp.where(is_sine, lon_total / 4, 0.0)
    fine_sin, fine_cos = sin_cos_of_phase(waves * k_fine + quarter, lon_total)
    coarse_rows = coarse.shape[1]
    k_coarse = lax.broadcasted_iota(jnp.int32, (coarse_rows, width), 0).astype(jnp.float32) * LANES
    coarse_sin, coarse_cos = sin_cos_of_phase(waves * k_coarse, lon_total)
    coarse[0] = coarse_sin
    coarse[1] = coarse_cos
    for a in range(coarse_count):
        block = coarse[1, pl.ds(a, 1), :] * fine_cos - coarse[0, pl.ds(a, 1), :] * fine_sin
        twiddle[pl.ds(a * LANES, LANES), :] = block.astype(jnp.bfloat16)

    row = lax.broadcasted_iota(jnp.int32, (LANES, LANES), 0)
    column = lax.broadcasted_iota(jnp.int32, (LANES, LANES), 1)
    turned = row + south * (LANES - 1 - 2 * row)
    order = (turned == column).astype(jnp.float32).astype(jnp.bfloat16)

    def flipped(d):
        index, bit = lat, 1
        while bit < lat_count:
            if d & bit:
                index = index + bit * (1 - 2 * ((lat // bit) % 2))
            bit *= 2
        return index

    def columns(q):
        low, high = chunk_tiles[q]
        return pl.ds(low * LANES, (high - low) * LANES)

    def remote(src, dst, sent_at, recv_at, device):
        return pltpu.make_async_remote_copy(
            src_ref=src, dst_ref=dst, send_sem=sent.at[sent_at], recv_sem=recv_at,
            device_id=device, device_id_type=MESH,
        )

    def y_group(d, q):
        if d < half_lats:
            return d
        return half_lats + 2 * (d - half_lats) + (q == chunk_count - 1)

    def pass_on(src, source_place, d, q):
        here = recv.at[fld, source_place, :, columns(q)]
        remote(src, here, 1, y_recv.at[y_group(d, q)], (lat, y_peer)).start()
        remote(src, here, 2, c_recv.at[source_place // half_lats], (lat, partner)).start()

    for q in range(chunk_count):
        low, high = chunk_tiles[q]
        rows = pl.ds(low * LANES, (high - low) * LANES)
        pltpu.make_async_copy(grid.at[rows], grid.at[rows], field_sem.at[q]).wait()
        spectra = jnp.dot(grid[rows, :], twiddle[...], preferred_element_type=jnp.float32)
        spectra = (spectra * (1.0 / lon_total)).astype(jnp.bfloat16)
        for t in range(low, high):
            part = spectra[(t - low) * LANES:(t - low + 1) * LANES, :]
            part = jnp.dot(order, part, preferred_element_type=jnp.float32)
            part = part.T
            for owner in range(lat_count):
                s0 = owner * slot_dev
                send[owner, :, pl.ds(t * LANES, LANES)] = jnp.concatenate(
                    [part[s0:s0 + slot_dev], part[slot_total + s0:slot_total + s0 + slot_dev]], axis=0
                ).astype(jnp.bfloat16)
        if q == 0:
            pl.semaphore_wait(barrier, lat_count + 1)
        for d in range(lat_count - 1, 0, -1):
            owner = flipped(d)
            remote(
                send.at[owner, :, columns(q)], recv.at[fld, place, :, columns(q)],
                0, lat_recv.at[d - 1, q], (owner, fld),
            ).start()
        pass_on(send.at[lat, :, columns(q)], place, 0, q)
        recv[fld, place, :, columns(q)] = send[lat, :, columns(q)]

    table_copy = pltpu.make_async_copy(legendre_ref, table, table_sem)
    table_copy.start()

    def hops(d):
        return (d & 1) + d // 2

    when = (2.2, 3.3, 4.4)
    events = []
    for d in range(lat_count):
        for q in range(chunk_count):
            arrival = when[q] + 1.45 * hops(d)
            if d:
                events.append((arrival, 0, d, q))
            if q == chunk_count - 1 or y_group(d, q) != y_group(d, q + 1):
                events.append((arrival + (1.9 if d else 2.4), 1, d, q))
    for _, kind, d, q in sorted(events):
        source = flipped(d)
        source_place = place_of(source)
        if kind == 0:
            here = recv.at[fld, source_place, :, columns(q)]
            remote(here, here, 0, lat_recv.at[d - 1, q], (lat, y_peer)).wait_recv()
            pass_on(here, source_place, d, q)
        else:
            members = [k for k in range(chunk_count) if y_group(d, k) == y_group(d, q)]
            low, high = chunk_tiles[members[0]][0], chunk_tiles[members[-1]][1]
            there = recv.at[y_peer, source_place, :, pl.ds(low * LANES, (high - low) * LANES)]
            remote(there, there, 1, y_recv.at[y_group(d, q)], (lat, y_peer)).wait_recv()
            remote(there, there, 3, d_recv.at[source_place // half_lats], (lat, partner)).start()

    depth = 2 * slot_dev
    pair_lats = 2 * lat_dev
    low_half = lax.broadcasted_iota(jnp.int32, (depth, LANES), 1) < HALF
    total_rows = 8 * depth
    trunc_total = 2 * row_dev * 4
    slot_of = lax.broadcasted_iota(jnp.int32, (row_dev, total_rows), 1) % slot_dev
    degree_row = 2 * (lax.broadcasted_iota(jnp.int32, (row_dev, total_rows), 0) + fld * row_dev)
    wave_of = jnp.zeros((1, total_rows), jnp.int32)
    for s in range(slot_dev):
        wave_of = jnp.where(slot_of[:1] == s, wave_smem[lat * slot_dev + s], wave_of)
    table_copy.wait()
    for h in range(half_lats // 2 - 1, -1, -1):
        for group, sem in ((partner, c_recv), (partner_y, d_recv)):
            block = recv.at[group, pl.ds(h * half_lats, half_lats)]
            remote(block, block, 3, sem.at[h], (lat, partner)).wait_recv()
        base = h * pair_lats
        for group in range(4):
            north = [recv[group, 2 * (2 * h + o)].astype(jnp.float32) for o in range(2)]
            mirror = [recv[group, 2 * (2 * h + o) + 1].astype(jnp.float32) for o in range(2)]
            for p in range(2):
                even_band, odd_band = [
                    n + m if p == 0 else n - m for n, m in zip(north, mirror)
                ]
                cut = main * LANES
                mid_even = even_band[:, cut:cut + LANES]
                mid_odd = odd_band[:, cut:cut + LANES]
                mid = (
                    jnp.where(low_half, mid_even, mid_odd),
                    pltpu.roll(jnp.where(low_half, mid_odd, mid_even), HALF, 1),
                )
                for f in range(2):
                    start = f * (cut + LANES)
                    rows = pl.ds((2 * group + f) * depth, depth)
                    folded[p, rows, pl.ds(base, cut)] = even_band[:, start:start + cut].astype(jnp.bfloat16)
                    folded[p, rows, pl.ds(base + cut, LANES)] = mid[f].astype(jnp.bfloat16)
                    folded[p, rows, pl.ds(base + cut + LANES, cut)] = odd_band[
                        :, start:start + cut
                    ].astype(jnp.bfloat16)
        for p in range(2):
            kept = jnp.zeros((row_dev, total_rows), jnp.float32)
            for s in range(slot_dev):
                sums = lax.dot_general(
                    table[s, p, :, pl.ds(base, pair_lats)], folded[p, :, pl.ds(base, pair_lats)],
                    (((1,), (1,)), ((), ())), preferred_element_type=jnp.float32,
                )
                kept = jnp.where(slot_of == s, sums, kept)
            if h > 0:
                partial[p] = kept
                continue
            kept = jnp.where(degree_row + (wave_of + p) <= trunc_total - 1, kept + partial[p], 0.0)
            padded = jnp.concatenate(
                [kept, jnp.zeros((spun.shape[1] * LANES - row_dev, total_rows), jnp.float32)], axis=0
            )
            for t in range(spun.shape[1]):
                spun[p, t] = padded[t * LANES:(t + 1) * LANES].T
    for s in range(slot_dev):
        for p in range(2):
            for c in range(2):
                for t in range(spun.shape[1]):
                    kept_rows = min(LANES, row_dev - t * LANES)
                    out_ref[s, pl.ds(p * 16 + c * 8, 8), pl.ds(t * LANES, kept_rows)] = spun[
                        p, t, pl.ds(c * slot_dev + s, 8, stride=depth), :
                    ][:, :kept_rows]
    for kind, count in ((0, lat_count - 1), (1, lat_count), (2, lat_count), (3, lat_count)):
        block = recv.at[fld, pl.ds(0, count)]
        remote(block, block, kind, table_sem, (lat, partner)).wait_send()


def shards_by_kernel(field_grid, wave_table, legendre):
    f_dev, lat_dev, lon_total = field_grid.shape
    slot_dev, _, row_dev, north_total = legendre.shape
    slot_total = wave_table.shape[0]
    lat_count = lax.axis_size("lat")
    rows = f_dev * lat_dev
    bf16, f32 = jnp.bfloat16, jnp.float32
    dma = pltpu.SemaphoreType.DMA
    padded_rows = -(-row_dev // LANES) * LANES
    coarse_rows = -(-(lon_total // LANES) // 8) * 8
    vmem, smem = pltpu.VMEM, pltpu.SMEM
    out = pl.pallas_call(
        functools.partial(transform_kernel, lat_count),
        out_shape=pltpu.VMEM((slot_dev, 32, row_dev), f32),
        in_specs=[pl.BlockSpec(memory_space=pl.ANY)] * 4,
        out_specs=pl.BlockSpec(memory_space=vmem),
        scratch_shapes=[
            vmem((rows, lon_total), bf16),
            vmem((lon_total, 2 * slot_total), bf16),
            vmem((2, coarse_rows, 2 * slot_total), f32),
            vmem(legendre.shape, bf16),
            vmem((lat_count, 2 * slot_dev, rows), bf16),
            vmem((4, lat_count, 2 * slot_dev, rows), bf16),
            vmem((2, 16 * slot_dev, north_total), bf16),
            vmem((2, row_dev, 16 * slot_dev), f32),
            vmem((2, padded_rows // LANES, 16 * slot_dev, LANES), f32),
            smem((slot_total,), jnp.int32),
            vmem((1, slot_total), jnp.int32),
            dma((3,)),
            dma((2,)),
            dma(()),
            dma((4,)),
            dma((lat_count - 1, 3)),
            dma((3 * lat_count // 2,)),
            dma((2,)),
            dma((2,)),
        ],
        compiler_params=pltpu.CompilerParams(
            collective_id=0, has_side_effects=True
        ),
    )(wave_table, wave_table.reshape(1, slot_total), field_grid, legendre)
    return jnp.transpose(out, (0, 2, 1))


def shards(field_grid, wave_table, legendre):
    f_dev, lat_dev, lon_total = field_grid.shape
    slot_dev, _, row_dev, _ = legendre.shape
    slot_total = wave_table.shape[0]
    fits = (
        f_dev == 2
        and slot_dev == 8
        and 2 * slot_total == LANES
        and lat_dev % LANES == HALF
        and lat_dev > LANES
        and lax.axis_size("fld") == 4
        and lax.axis_size("lat") == 8
        and lon_total % LANES == 0
        and row_dev % 8 == 0
        and 2 * row_dev * 4 * lon_total < 2**24
    )
    if fits:
        return shards_by_kernel(field_grid, wave_table, legendre)
    return shards_by_collectives(field_grid, wave_table, legendre)


def solution(mesh):
    placed = (P("fld", "lat", None), P(), P("lat", None, "fld", None))
    return jax.shard_map(
        shards, mesh=mesh, in_specs=placed, out_specs=P("lat", "fld", None), check_vma=False
    )
```

profile of v0, /device:TPU:0, one launch (start us, length us, event | category | flops | bytes accessed | tf_op | source)
XLA Modules:
  0.0 20.8 jit_solution(10945958972405528592)
XLA Ops:
  0.0 20.1 %shard_map.37 = f32[8,32,160]{2,1,0:T(8,128)S(1)} custom-call(s32[64]{0:T(128)} %wave_hbm.1, s32[1,64]{1,0:T(1,128)} %bitcast.3, bf16[2,320,5120]{2,1,0:T(8,128)(2,1)} %field_ref.1, bf16[8,2,160,1280]{3,2,1,0:T(8,128)(2,1)} %legendre_ref.1), custom_call_target="tpu_custom_call" | custom-call | tf_op jit(solution)/shard_map/pallas_call | solution.py:373
  20.1 0.7 %copy.5 = f32[8,160,32]{1,2,0:T(8,128)} copy(f32[8,160,32]{1,2,0:T(8,128)S(1)} %bitcast.2) | data formatting | bytes 327680
where the time goes:
time: 20.9 us; the launch traced here: 20.8 us
  Pallas kernels  20.1 us (96%)
  local copies, waits for them, and re-layouts  0.71 us (3%)
    pallas_call x1, Pallas kernels, shards_by_kernel(): pl.pallas_call(functools.partial(transform_kernel, lat_count), out_shape=...  20.1 us
    unnamed x1, local copies, waits for them, and re-layouts  0.71 us

commit v1 on v0

--- a/solution.py
+++ b/solution.py
@@ -81,7 +81,14 @@
 LANES = 128
 HALF = 64
 MESH = pl.DeviceIdType.MESH
-
+ARRIVALS = (
+    (1, 1, 0), (1, 2, 0), (0, 0, 0), (0, 0, 1), (0, 1, 0), (0, 2, 0),
+    (1, 3, 0), (1, 1, 1), (1, 4, 0), (1, 2, 1), (1, 5, 0), (0, 3, 0),
+    (0, 1, 1), (1, 6, 0), (0, 4, 0), (1, 3, 1), (0, 2, 1), (0, 5, 0),
+    (1, 7, 0), (0, 6, 0), (1, 4, 1), (0, 3, 1), (1, 5, 1), (0, 7, 0),
+    (1, 6, 1), (0, 4, 1), (1, 7, 1), (0, 5, 1), (0, 6, 1), (0, 7, 1),
+)
+STRAIGHT = ((4, 1), (5, 1))
 
 def sin_cos_of_phase(phase, period):
     turns = jnp.floor(phase * (1.0 / period))
@@ -113,13 +120,14 @@
 def transform_kernel(
     lat_count, wave_hbm, wave_row_hbm, field_ref, legendre_ref, out_ref,
     grid, twiddle, coarse, table, send, recv, folded, partial, spun, wave_smem, wave_row,
-    field_sem, wave_sem, table_sem, sent, lat_recv, y_recv, c_recv, d_recv,
+    field_sem, wave_sem, table_sem, sent, came,
 ):
     lat = lax.axis_index("lat")
     fld = lax.axis_index("fld")
-    y_peer = (fld + 2) % 4
     partner = fld + 1 - 2 * (fld % 2)
-    partner_y = (partner + 2) % 4
+    core = fld % 2
+    hub = fld + 1 - core
+    hub_y = (hub + 2) % 4
 
     _, lat_dev, lon_total = field_ref.shape
     main = lat_dev // LANES
@@ -177,12 +185,21 @@
         load_main(1, t, main + 1 + t)
 
     barrier = pltpu.get_barrier_semaphore()
-    for d in range(1, lat_count):
-        pl.semaphore_signal(
-            barrier, inc=1, device_id=((lat + d) % lat_count, fld), device_id_type=MESH
-        )
-    for other in (y_peer, partner):
-        pl.semaphore_signal(barrier, inc=1, device_id=(lat, other), device_id_type=MESH)
+
+    @pl.when(core == 1)
+    def _():
+        for d in range(1, lat_count):
+            for c in range(2):
+                pl.semaphore_signal(
+                    barrier, inc=1, device_id=((lat + d) % lat_count, hub - c), device_id_type=MESH
+                )
+        pl.semaphore_signal(barrier, inc=1, device_id=(lat, hub_y), device_id_type=MESH)
+
+    @pl.when(core == 0)
+    def _():
+        pl.semaphore_signal(barrier, inc=1, device_id=(lat, hub_y), device_id_type=MESH)
+
+    pl.semaphore_signal(barrier, inc=1, device_id=(lat, partner), device_id_type=MESH)
 
     for copy in wave_copies:
         copy.wait()
@@ -226,15 +243,75 @@
             device_id=device, device_id_type=MESH,
         )
 
-    def y_group(d, q):
-        if d < half_lats:
-            return d
-        return half_lats + 2 * (d - half_lats) + (q == chunk_count - 1)
-
-    def pass_on(src, source_place, d, q):
-        here = recv.at[fld, source_place, :, columns(q)]
-        remote(src, here, 1, y_recv.at[y_group(d, q)], (lat, y_peer)).start()
-        remote(src, here, 2, c_recv.at[source_place // half_lats], (lat, partner)).start()
+    middle = (lat // 2 + lat // 4) % 2
+    came_from = 2 * lat_count * 2
+
+    def peer(e):
+        index = flipped(e)
+        if e < half_lats:
+            return index, e
+        turned = middle * (1 - 2 * ((index // 2) % 2))
+        return index + 2 * turned, e + 2 * middle * (1 - 2 * ((e // 2) % 2))
+
+    def lat_sem(c, d, q):
+        return came.at[(c * lat_count + d) * 2 + (q == chunk_count - 1)]
+
+    def y_sem(c, e, part):
+        pair = e // 2
+        split = pair + part * (half_lats // 2) if 2 * pair >= half_lats else pair
+        return came.at[came_from + c * (half_lats + half_lats // 2) + split]
+
+    def even_sem(h, group):
+        return came.at[h * 4 + group]
+
+    def part_columns(part):
+        low = chunk_tiles[-1][0] if part else 0
+        high = tiles if part else chunk_tiles[-1][0]
+        return pl.ds(low * LANES, (high - low) * LANES)
+
+    def pass_on(src, group, source_place, c, e, where, part=0):
+        there = recv.at[group, source_place, :, where]
+        remote(src, there, 1, y_sem(c, e, part), (lat, hub_y)).start()
+        if (e, part) in STRAIGHT:
+            remote(
+                src, there, 1, even_sem(source_place // half_lats, group), (lat, hub_y - 1)
+            ).start()
+        remote(src, there, 2, even_sem(source_place // half_lats, group), (lat, partner)).start()
+
+    def send_chunk(q):
+        for e in range(lat_count - 1, 0, -1):
+            owner, d = peer(e)
+            remote(
+                send.at[owner, :, columns(q)], recv.at[fld, place, :, columns(q)],
+                0, lat_sem(core, d, q), (owner, hub),
+            ).start()
+
+        @pl.when(core == 1)
+        def _():
+            pass_on(send.at[lat, :, columns(q)], fld, place, 1, 0, columns(q))
+            recv[fld, place, :, columns(q)] = send[lat, :, columns(q)]
+
+        @pl.when(core == 0)
+        def _():
+            remote(
+                send.at[lat, :, columns(q)], recv.at[fld, place, :, columns(q)],
+                2, lat_sem(0, 0, q), (lat, partner),
+            ).start()
+
+    patience = jnp.maximum(chunk_count - 1 - (lat // 2 + lat % 2), 0)
+    greeted = lat_count + 2 * core
+
+    def release(q):
+        @pl.when(patience == q)
+        def _():
+            pl.semaphore_wait(barrier, greeted)
+            for k in range(q + 1):
+                send_chunk(k)
+
+        if q > 0:
+            @pl.when(patience < q)
+            def _():
+                send_chunk(q)
 
     for q in range(chunk_count):
         low, high = chunk_tiles[q]
@@ -251,45 +328,42 @@
                 send[owner, :, pl.ds(t * LANES, LANES)] = jnp.concatenate(
                     [part[s0:s0 + slot_dev], part[slot_total + s0:slot_total + s0 + slot_dev]], axis=0
                 ).astype(jnp.bfloat16)
-        if q == 0:
-            pl.semaphore_wait(barrier, lat_count + 1)
-        for d in range(lat_count - 1, 0, -1):
-            owner = flipped(d)
-            remote(
-                send.at[owner, :, columns(q)], recv.at[fld, place, :, columns(q)],
-                0, lat_recv.at[d - 1, q], (owner, fld),
-            ).start()
-        pass_on(send.at[lat, :, columns(q)], place, 0, q)
-        recv[fld, place, :, columns(q)] = send[lat, :, columns(q)]
+        release(q)
 
     table_copy = pltpu.make_async_copy(legendre_ref, table, table_sem)
     table_copy.start()
 
-    def hops(d):
-        return (d & 1) + d // 2
-
-    when = (2.2, 3.3, 4.4)
-    events = []
-    for d in range(lat_count):
-        for q in range(chunk_count):
-            arrival = when[q] + 1.45 * hops(d)
-            if d:
-                events.append((arrival, 0, d, q))
-            if q == chunk_count - 1 or y_group(d, q) != y_group(d, q + 1):
-                events.append((arrival + (1.9 if d else 2.4), 1, d, q))
-    for _, kind, d, q in sorted(events):
-        source = flipped(d)
+    def relay(c, e, part):
+        source, d = peer(e)
+        group = hub - 1 + c
         source_place = place_of(source)
-        if kind == 0:
-            here = recv.at[fld, source_place, :, columns(q)]
-            remote(here, here, 0, lat_recv.at[d - 1, q], (lat, y_peer)).wait_recv()
-            pass_on(here, source_place, d, q)
-        else:
-            members = [k for k in range(chunk_count) if y_group(d, k) == y_group(d, q)]
-            low, high = chunk_tiles[members[0]][0], chunk_tiles[members[-1]][1]
-            there = recv.at[y_peer, source_place, :, pl.ds(low * LANES, (high - low) * LANES)]
-            remote(there, there, 1, y_recv.at[y_group(d, q)], (lat, y_peer)).wait_recv()
-            remote(there, there, 3, d_recv.at[source_place // half_lats], (lat, partner)).start()
+        here = recv.at[group, source_place, :, part_columns(part)]
+        remote(here, here, 0, lat_sem(c, d, (chunk_count - 1) * part), (lat, partner)).wait_recv()
+        pass_on(here, group, source_place, c, e, part_columns(part), part)
+
+    def hand_over(c, pair, part=None):
+        group = hub_y - 1 + c
+        where = pl.ds(0, tiles * LANES) if part is None else part_columns(part)
+        both = recv.at[group, pl.ds(0, 2), :, where]
+        remote(both, both, 1, y_sem(c, 2 * pair, part or 0), (lat, hub_y)).wait_recv()
+        for e in (2 * pair, 2 * pair + 1):
+            if (e, part) not in STRAIGHT:
+                source_place = place_of(peer(e)[0])
+                there = recv.at[group, source_place, :, where]
+                remote(
+                    there, there, 2, even_sem(source_place // half_lats, group), (lat, partner)
+                ).start()
+
+    def gather(*parts):
+        for pair, part in parts:
+            for c in (1, 0):
+                hand_over(c, pair, part)
+
+    @pl.when(core == 1)
+    def _():
+        for c, e, part in ARRIVALS:
+            relay(c, e, part)
+        gather((0, None), (1, None), (2, 0), (3, 0), (2, 1))
 
     depth = 2 * slot_dev
     pair_lats = 2 * lat_dev
@@ -303,9 +377,12 @@
         wave_of = jnp.where(slot_of[:1] == s, wave_smem[lat * slot_dev + s], wave_of)
     table_copy.wait()
     for h in range(half_lats // 2 - 1, -1, -1):
-        for group, sem in ((partner, c_recv), (partner_y, d_recv)):
-            block = recv.at[group, pl.ds(h * half_lats, half_lats)]
-            remote(block, block, 3, sem.at[h], (lat, partner)).wait_recv()
+        @pl.when(core == 0)
+        def _():
+            for group in range(4):
+                block = recv.at[group, pl.ds(h * half_lats, half_lats)]
+                remote(block, block, 2, even_sem(h, group), (lat, partner)).wait_recv()
+
         base = h * pair_lats
         for group in range(4):
             north = [recv[group, 2 * (2 * h + o)].astype(jnp.float32) for o in range(2)]
@@ -330,13 +407,19 @@
                         :, start:start + cut
                     ].astype(jnp.bfloat16)
         for p in range(2):
+            if h > 0 and p == 1:
+                @pl.when(core == 1)
+                def _():
+                    gather((3, 1))
             kept = jnp.zeros((row_dev, total_rows), jnp.float32)
-            for s in range(slot_dev):
+            for first in range(0, slot_dev, 2):
                 sums = lax.dot_general(
-                    table[s, p, :, pl.ds(base, pair_lats)], folded[p, :, pl.ds(base, pair_lats)],
+                    table[first:first + 2, p, :, pl.ds(base, pair_lats)].reshape(2 * row_dev, pair_lats),
+                    folded[p, :, pl.ds(base, pair_lats)],
                     (((1,), (1,)), ((), ())), preferred_element_type=jnp.float32,
                 )
-                kept = jnp.where(slot_of == s, sums, kept)
+                for s in range(2):
+                    kept = jnp.where(slot_of == first + s, sums[s * row_dev:(s + 1) * row_dev], kept)
             if h > 0:
                 partial[p] = kept
                 continue
@@ -354,9 +437,25 @@
                     out_ref[s, pl.ds(p * 16 + c * 8, 8), pl.ds(t * LANES, kept_rows)] = spun[
                         p, t, pl.ds(c * slot_dev + s, 8, stride=depth), :
                     ][:, :kept_rows]
-    for kind, count in ((0, lat_count - 1), (1, lat_count), (2, lat_count), (3, lat_count)):
-        block = recv.at[fld, pl.ds(0, count)]
+    def drain(kind, block):
         remote(block, block, kind, table_sem, (lat, partner)).wait_send()
+
+    drain(0, recv.at[fld, pl.ds(0, lat_count - 1)])
+
+    @pl.when(core == 1)
+    def _():
+        straight = 2 * len(STRAIGHT)
+        drain(1, recv.at[pl.ds(0, 2)])
+        drain(2, recv.at[pl.ds(0, 3)])
+        if straight:
+            drain(1, recv.at[0, pl.ds(0, straight), :, part_columns(1)])
+        if straight < lat_count:
+            drain(2, recv.at[0, pl.ds(straight, lat_count - straight), :, part_columns(1)])
+        drain(2, recv.at[0, :, :, part_columns(0)])
+
+    @pl.when(core == 0)
+    def _():
+        drain(2, recv.at[0, 0])
 
 
 def shards_by_kernel(field_grid, wave_table, legendre):
@@ -390,11 +489,8 @@
             dma((3,)),
             dma((2,)),
             dma(()),
-            dma((4,)),
-            dma((lat_count - 1, 3)),
-            dma((3 * lat_count // 2,)),
-            dma((2,)),
-            dma((2,)),
+            dma((3,)),
+            dma((5 * lat_count + lat_count // 2,)),
         ],
         compiler_params=pltpu.CompilerParams(
             collective_id=0, has_side_effects=True

time: 20.9 us -> 17.6 us (0.84)
  Pallas kernels: 20.1 us -> 16.8 us
    pallas_call x1, Pallas kernels: 20.1 us -> 16.8 us  [shards_by_kernel(): pl.pallas_call(functools.partial(transform_kernel, lat_count), out_shape=...]
where the time goes in v1:
time: 17.6 us; the launch traced here: 17.5 us
  Pallas kernels  16.8 us (95%)
  local copies, waits for them, and re-layouts  0.71 us (4%)
    pallas_call x1, Pallas kernels, shards_by_kernel(): pl.pallas_call(functools.partial(transform_kernel, lat_count), out_shape=...  16.8 us
    unnamed x1, local copies, waits for them, and re-layouts  0.71 us

profile of v1, /device:TPU:0, one launch (start us, length us, event | category | flops | bytes accessed | tf_op | source)
XLA Modules:
  0.0 17.5 jit_solution(962145542856788381)
XLA Ops:
  0.0 16.8 %shard_map.37 = f32[8,32,160]{2,1,0:T(8,128)S(1)} custom-call(s32[64]{0:T(128)} %wave_hbm.1, s32[1,64]{1,0:T(1,128)} %bitcast.3, bf16[2,320,5120]{2,1,0:T(8,128)(2,1)} %field_ref.1, bf16[8,2,160,1280]{3,2,1,0:T(8,128)(2,1)} %legendre_ref.1), custom_call_target="tpu_custom_call" | custom-call | tf_op jit(solution)/shard_map/pallas_call | solution.py:472
  16.8 0.7 %copy.5 = f32[8,160,32]{1,2,0:T(8,128)} copy(f32[8,160,32]{1,2,0:T(8,128)S(1)} %bitcast.2) | data formatting | bytes 327680

commit v2 on v1

--- a/solution.py
+++ b/solution.py
@@ -82,13 +82,13 @@
 HALF = 64
 MESH = pl.DeviceIdType.MESH
 ARRIVALS = (
-    (1, 1, 0), (1, 2, 0), (0, 0, 0), (0, 0, 1), (0, 1, 0), (0, 2, 0),
-    (1, 3, 0), (1, 1, 1), (1, 4, 0), (1, 2, 1), (1, 5, 0), (0, 3, 0),
-    (0, 1, 1), (1, 6, 0), (0, 4, 0), (1, 3, 1), (0, 2, 1), (0, 5, 0),
-    (1, 7, 0), (0, 6, 0), (1, 4, 1), (0, 3, 1), (1, 5, 1), (0, 7, 0),
-    (1, 6, 1), (0, 4, 1), (1, 7, 1), (0, 5, 1), (0, 6, 1), (0, 7, 1),
+    (1, 1, 0), (1, 2, 0), (0, 0, 0), (0, 0, 1), (0, 1, 0), (1, 3, 0),
+    (1, 4, 0), (1, 1, 1), (0, 2, 0), (1, 2, 1), (0, 3, 0), (1, 5, 0),
+    (0, 1, 1), (1, 6, 0), (0, 2, 1), (1, 3, 1), (0, 4, 0), (1, 4, 1),
+    (0, 5, 0), (0, 3, 1), (0, 6, 0), (1, 7, 0), (1, 6, 1), (1, 5, 1),
+    (0, 4, 1), (0, 7, 0), (0, 6, 1), (1, 7, 1), (0, 5, 1), (0, 7, 1),
 )
-STRAIGHT = ((4, 1), (5, 1))
+STRAIGHT = ()
 
 def sin_cos_of_phase(phase, period):
     turns = jnp.floor(phase * (1.0 / period))
@@ -128,6 +128,10 @@
     core = fld % 2
     hub = fld + 1 - core
     hub_y = (hub + 2) % 4
+    side = fld // 2
+    first_chip = (lat == 0) & (side == 0)
+    across = (lat == 0) & (side == 1)
+    far = (lat >= lat_count // 2) & (fld == 2)
 
     _, lat_dev, lon_total = field_ref.shape
     main = lat_dev // LANES
@@ -200,6 +204,11 @@
         pl.semaphore_signal(barrier, inc=1, device_id=(lat, hub_y), device_id_type=MESH)
 
     pl.semaphore_signal(barrier, inc=1, device_id=(lat, partner), device_id_type=MESH)
+
+    @pl.when(first_chip & (core == 1))
+    def _():
+        for other in range(half_lats, lat_count):
+            pl.semaphore_signal(barrier, inc=1, device_id=(other, 2), device_id_type=MESH)
 
     for copy in wave_copies:
         copy.wait()
@@ -244,7 +253,7 @@
         )
 
     middle = (lat // 2 + lat // 4) % 2
-    came_from = 2 * lat_count * 2
+    came_from = 4 * lat_count - 2
 
     def peer(e):
         index = flipped(e)
@@ -254,29 +263,46 @@
         return index + 2 * turned, e + 2 * middle * (1 - 2 * ((e // 2) % 2))
 
     def lat_sem(c, d, q):
-        return came.at[(c * lat_count + d) * 2 + (q == chunk_count - 1)]
+        return came.at[(c * (lat_count - 1) + d) * 2 + (q == chunk_count - 1)]
 
     def y_sem(c, e, part):
-        pair = e // 2
-        split = pair + part * (half_lats // 2) if 2 * pair >= half_lats else pair
-        return came.at[came_from + c * (half_lats + half_lats // 2) + split]
-
-    def even_sem(h, group):
-        return came.at[h * 4 + group]
+        if isinstance(e, int) and e < half_lats:
+            split = 0
+        else:
+            split = e // 2 - half_lats // 2 + 1 + 2 * part
+        return came.at[came_from + c * 5 + split]
+
+    def even_sem(source_place, part, group):
+        if part == 0:
+            return came.at[group]
+        return came.at[4 * (1 - source_place // half_lats) + group]
 
     def part_columns(part):
         low = chunk_tiles[-1][0] if part else 0
         high = tiles if part else chunk_tiles[-1][0]
         return pl.ds(low * LANES, (high - low) * LANES)
 
+    def straight_from_source(c, e, part):
+        return c == 0 and e >= half_lats and part == 1
+
+    def unless(skipped, chip, action):
+        if skipped:
+            pl.when(jnp.logical_not(chip))(action)
+        else:
+            action()
+
     def pass_on(src, group, source_place, c, e, where, part=0):
         there = recv.at[group, source_place, :, where]
-        remote(src, there, 1, y_sem(c, e, part), (lat, hub_y)).start()
-        if (e, part) in STRAIGHT:
-            remote(
-                src, there, 1, even_sem(source_place // half_lats, group), (lat, hub_y - 1)
-            ).start()
-        remote(src, there, 2, even_sem(source_place // half_lats, group), (lat, partner)).start()
+
+        def cross():
+            remote(src, there, 1, y_sem(c, e, part * (e >= half_lats)), (lat, hub_y)).start()
+            if (c, e, part) in STRAIGHT:
+                remote(
+                    src, there, 1, even_sem(source_place, part, group), (lat, hub_y - 1)
+                ).start()
+
+        unless(straight_from_source(c, e, part), across, cross)
+        remote(src, there, 2, even_sem(source_place, part, group), (lat, partner)).start()
 
     def send_chunk(q):
         for e in range(lat_count - 1, 0, -1):
@@ -286,9 +312,15 @@
                 0, lat_sem(core, d, q), (owner, hub),
             ).start()
 
+        if q == chunk_count - 1:
+            @pl.when(far)
+            def _():
+                block = recv.at[fld, place, :, columns(q)]
+                remote(send.at[0, :, columns(q)], block, 0, y_sem(0, lat, 1), (0, 1)).start()
+
         @pl.when(core == 1)
         def _():
-            pass_on(send.at[lat, :, columns(q)], fld, place, 1, 0, columns(q))
+            pass_on(send.at[lat, :, columns(q)], fld, place, 1, 0, columns(q), int(q == chunk_count - 1))
             recv[fld, place, :, columns(q)] = send[lat, :, columns(q)]
 
         @pl.when(core == 0)
@@ -299,7 +331,7 @@
             ).start()
 
     patience = jnp.maximum(chunk_count - 1 - (lat // 2 + lat % 2), 0)
-    greeted = lat_count + 2 * core
+    greeted = lat_count + 2 * core + far.astype(jnp.int32)
 
     def release(q):
         @pl.when(patience == q)
@@ -330,8 +362,19 @@
                 ).astype(jnp.bfloat16)
         release(q)
 
-    table_copy = pltpu.make_async_copy(legendre_ref, table, table_sem)
-    table_copy.start()
+    cut = main * LANES
+    pair_lats = 2 * lat_dev
+    spans = (
+        (cut, 0, LANES),
+        (pair_lats, LANES, pair_lats),
+        (0, pair_lats + LANES, cut),
+        (cut + LANES, pair_lats + LANES + cut, cut),
+    )
+    for source, target, count in spans:
+        pltpu.make_async_copy(
+            legendre_ref.at[:, :, :, pl.ds(source, count)],
+            table.at[:, :, :, pl.ds(target, count)], table_sem,
+        ).start()
 
     def relay(c, e, part):
         source, d = peer(e)
@@ -344,29 +387,32 @@
     def hand_over(c, pair, part=None):
         group = hub_y - 1 + c
         where = pl.ds(0, tiles * LANES) if part is None else part_columns(part)
-        both = recv.at[group, pl.ds(0, 2), :, where]
+        members = range(half_lats) if pair == 0 else (2 * pair, 2 * pair + 1)
+        both = recv.at[group, pl.ds(0, len(members)), :, where]
         remote(both, both, 1, y_sem(c, 2 * pair, part or 0), (lat, hub_y)).wait_recv()
-        for e in (2 * pair, 2 * pair + 1):
-            if (e, part) not in STRAIGHT:
-                source_place = place_of(peer(e)[0])
-                there = recv.at[group, source_place, :, where]
-                remote(
-                    there, there, 2, even_sem(source_place // half_lats, group), (lat, partner)
-                ).start()
+        for e in members:
+            source_place = place_of(peer(e)[0])
+            for k in (0, 1) if part is None else (part,):
+                if (c, e, k) in STRAIGHT:
+                    continue
+                there = recv.at[group, source_place, :, part_columns(k)]
+                hand = remote(there, there, 2, even_sem(source_place, k, group), (lat, partner))
+                hand.start()
 
     def gather(*parts):
-        for pair, part in parts:
-            for c in (1, 0):
-                hand_over(c, pair, part)
+        for c, pair, part in parts:
+            hand_over(c, pair, part)
 
     @pl.when(core == 1)
     def _():
         for c, e, part in ARRIVALS:
             relay(c, e, part)
-        gather((0, None), (1, None), (2, 0), (3, 0), (2, 1))
+        gather(
+            (1, 2, 0), (0, 2, 0), (1, 0, None), (0, 0, None), (1, 3, 0), (1, 2, 1),
+            (0, 3, 0), (0, 2, 1),
+        )
 
     depth = 2 * slot_dev
-    pair_lats = 2 * lat_dev
     low_half = lax.broadcasted_iota(jnp.int32, (depth, LANES), 1) < HALF
     total_rows = 8 * depth
     trunc_total = 2 * row_dev * 4
@@ -375,52 +421,73 @@
     wave_of = jnp.zeros((1, total_rows), jnp.int32)
     for s in range(slot_dev):
         wave_of = jnp.where(slot_of[:1] == s, wave_smem[lat * slot_dev + s], wave_of)
-    table_copy.wait()
-    for h in range(half_lats // 2 - 1, -1, -1):
+    pltpu.make_async_copy(table, table, table_sem).wait()
+    widths = (pair_lats + LANES, 2 * cut)
+
+    def fold(h, keep):
+        for group in range(4):
+            north = [recv[group, 2 * (2 * h + o), :, keep].astype(jnp.float32) for o in range(2)]
+            mirror = [recv[group, 2 * (2 * h + o) + 1, :, keep].astype(jnp.float32) for o in range(2)]
+            for p in range(2):
+                yield group, p, [n + m if p == 0 else n - m for n, m in zip(north, mirror)]
+
+    def put(group, p, f, start, value):
+        rows = pl.ds((2 * group + f) * depth, depth)
+        folded[p, rows, pl.ds(start, value.shape[1])] = value.astype(jnp.bfloat16)
+
+    def put_middle(group, p, bands, start):
+        mid_even, mid_odd = bands
+        put(group, p, 0, start, jnp.where(low_half, mid_even, mid_odd))
+        put(
+            group, p, 1, start,
+            pltpu.roll(jnp.where(low_half, mid_odd, mid_even), HALF, 1),
+        )
+
+    for phase in range(2):
+        base = phase * widths[0]
         @pl.when(core == 0)
         def _():
             for group in range(4):
-                block = recv.at[group, pl.ds(h * half_lats, half_lats)]
-                remote(block, block, 2, even_sem(h, group), (lat, partner)).wait_recv()
-
-        base = h * pair_lats
-        for group in range(4):
-            north = [recv[group, 2 * (2 * h + o)].astype(jnp.float32) for o in range(2)]
-            mirror = [recv[group, 2 * (2 * h + o) + 1].astype(jnp.float32) for o in range(2)]
-            for p in range(2):
-                even_band, odd_band = [
-                    n + m if p == 0 else n - m for n, m in zip(north, mirror)
-                ]
-                cut = main * LANES
-                mid_even = even_band[:, cut:cut + LANES]
-                mid_odd = odd_band[:, cut:cut + LANES]
-                mid = (
-                    jnp.where(low_half, mid_even, mid_odd),
-                    pltpu.roll(jnp.where(low_half, mid_odd, mid_even), HALF, 1),
-                )
+                if phase == 0:
+                    block = recv.at[group, :, :, pl.ds(0, (tiles + main + 1) // 2 * LANES)]
+                else:
+                    block = recv.at[group, pl.ds(0, half_lats), :, part_columns(1)]
+                remote(block, block, 2, came.at[4 * phase + group], (lat, partner)).wait_recv()
+
+        if phase == 0:
+            for group, p, bands in fold(0, pl.ds(cut, LANES)):
+                put_middle(group, p, bands, 0)
+            for group, p, (even_band, odd_band) in fold(1, slice(None)):
                 for f in range(2):
                     start = f * (cut + LANES)
-                    rows = pl.ds((2 * group + f) * depth, depth)
-                    folded[p, rows, pl.ds(base, cut)] = even_band[:, start:start + cut].astype(jnp.bfloat16)
-                    folded[p, rows, pl.ds(base + cut, LANES)] = mid[f].astype(jnp.bfloat16)
-                    folded[p, rows, pl.ds(base + cut + LANES, cut)] = odd_band[
-                        :, start:start + cut
-                    ].astype(jnp.bfloat16)
+                    put(group, p, f, LANES, even_band[:, start:start + cut])
+                    put(group, p, f, LANES + cut + LANES, odd_band[:, start:start + cut])
+                put_middle(
+                    group, p, [band[:, cut:cut + LANES] for band in (even_band, odd_band)], LANES + cut
+                )
+        else:
+            for f in range(2):
+                for group, p, bands in fold(0, pl.ds(f * (cut + LANES), cut)):
+                    for o in range(2):
+                        put(group, p, f, base + o * cut, bands[o])
         for p in range(2):
-            if h > 0 and p == 1:
+            if phase == 0 and p == 1:
                 @pl.when(core == 1)
                 def _():
-                    gather((3, 1))
+                    gather((1, 3, 1), (0, 3, 1))
+
             kept = jnp.zeros((row_dev, total_rows), jnp.float32)
             for first in range(0, slot_dev, 2):
                 sums = lax.dot_general(
-                    table[first:first + 2, p, :, pl.ds(base, pair_lats)].reshape(2 * row_dev, pair_lats),
-                    folded[p, :, pl.ds(base, pair_lats)],
+                    table[first:first + 2, p, :, pl.ds(base, widths[phase])].reshape(
+                        2 * row_dev, widths[phase]
+                    ),
+                    folded[p, :, pl.ds(base, widths[phase])],
                     (((1,), (1,)), ((), ())), preferred_element_type=jnp.float32,
                 )
                 for s in range(2):
                     kept = jnp.where(slot_of == first + s, sums[s * row_dev:(s + 1) * row_dev], kept)
-            if h > 0:
+            if phase == 0:
                 partial[p] = kept
                 continue
             kept = jnp.where(degree_row + (wave_of + p) <= trunc_total - 1, kept + partial[p], 0.0)
@@ -442,16 +509,30 @@
 
     drain(0, recv.at[fld, pl.ds(0, lat_count - 1)])
 
+    @pl.when(far)
+    def _():
+        drain(0, recv.at[0, 0, :, part_columns(1)])
+
     @pl.when(core == 1)
     def _():
-        straight = 2 * len(STRAIGHT)
-        drain(1, recv.at[pl.ds(0, 2)])
-        drain(2, recv.at[pl.ds(0, 3)])
-        if straight:
-            drain(1, recv.at[0, pl.ds(0, straight), :, part_columns(1)])
-        if straight < lat_count:
-            drain(2, recv.at[0, pl.ds(straight, lat_count - straight), :, part_columns(1)])
-        drain(2, recv.at[0, :, :, part_columns(0)])
+        def drain_parts(kind, chip, events):
+            for part in range(2):
+                where = part_columns(part)
+                skipped = [v for v in events if v[2] == part and straight_from_source(*v)]
+                others = skipped if chip is not None else []
+                always = [v for v in events if v[2] == part and v not in others]
+                for start in range(0, len(always), lat_count):
+                    count = min(lat_count, len(always) - start)
+                    drain(kind, recv.at[0, pl.ds(0, count), :, where])
+                if others:
+                    @pl.when(jnp.logical_not(chip))
+                    def _():
+                        drain(kind, recv.at[0, pl.ds(0, len(others)), :, where])
+
+        pieces = [(c, e, part) for c in range(2) for e in range(lat_count) for part in range(2)]
+        drain_parts(1, across, pieces + list(STRAIGHT))
+        drain(2, recv.at[pl.ds(0, 2)])
+        drain_parts(2, None, [v for v in pieces if v not in STRAIGHT])
 
     @pl.when(core == 0)
     def _():
@@ -490,7 +571,7 @@
             dma((2,)),
             dma(()),
             dma((3,)),
-            dma((5 * lat_count + lat_count // 2,)),
+            dma((4 * lat_count + 8,)),
         ],
         compiler_params=pltpu.CompilerParams(
             collective_id=0, has_side_effects=True
@@ -508,6 +589,7 @@
         and slot_dev == 8
         and 2 * slot_total == LANES
         and lat_dev % LANES == HALF
+        and lat_dev // LANES % 2 == 0
         and lat_dev > LANES
         and lax.axis_size("fld") == 4
         and lax.axis_size("lat") == 8

time: 17.6 us -> 17.6 us (level)
  no operation moved by 1% of the time
where the time goes in v2:
time: 17.6 us; the launch traced here: 17.4 us
  Pallas kernels  16.7 us (95%)
  local copies, waits for them, and re-layouts  0.71 us (4%)
    pallas_call x1, Pallas kernels, shards_by_kernel(): pl.pallas_call(functools.partial(transform_kernel, lat_count), out_shape=...  16.7 us
    unnamed x1, local copies, waits for them, and re-layouts  0.71 us

profile of v2, /device:TPU:0, one launch (start us, length us, event | category | flops | bytes accessed | tf_op | source)
XLA Modules:
  0.0 17.4 jit_solution(8771425905842694064)
XLA Ops:
  0.0 16.7 %shard_map.37 = f32[8,32,160]{2,1,0:T(8,128)S(1)} custom-call(s32[64]{0:T(128)} %wave_hbm.1, s32[1,64]{1,0:T(1,128)} %bitcast.3, bf16[2,320,5120]{2,1,0:T(8,128)(2,1)} %field_ref.1, bf16[8,2,160,1280]{3,2,1,0:T(8,128)(2,1)} %legendre_ref.1), custom_call_target="tpu_custom_call" | custom-call | tf_op jit(solution)/shard_map/pallas_call | solution.py:553
  16.7 0.7 %copy.5 = f32[8,160,32]{1,2,0:T(8,128)} copy(f32[8,160,32]{1,2,0:T(8,128)S(1)} %bitcast.2) | data formatting | bytes 327680

commit v3 on v2

--- a/solution.py
+++ b/solution.py
@@ -210,8 +210,7 @@
         for other in range(half_lats, lat_count):
             pl.semaphore_signal(barrier, inc=1, device_id=(other, 2), device_id_type=MESH)
 
-    for copy in wave_copies:
-        copy.wait()
+    wave_copies[0].wait()
     waves = wave_row[...].astype(jnp.float32)
     waves = jnp.concatenate([waves, waves], axis=1)
     width = 2 * slot_total
@@ -418,6 +417,7 @@
     trunc_total = 2 * row_dev * 4
     slot_of = lax.broadcasted_iota(jnp.int32, (row_dev, total_rows), 1) % slot_dev
     degree_row = 2 * (lax.broadcasted_iota(jnp.int32, (row_dev, total_rows), 0) + fld * row_dev)
+    wave_copies[1].wait()
     wave_of = jnp.zeros((1, total_rows), jnp.int32)
     for s in range(slot_dev):
         wave_of = jnp.where(slot_of[:1] == s, wave_smem[lat * slot_dev + s], wave_of)

time: 17.6 us -> 17.6 us (level)
  no operation moved by 1% of the time
where the time goes in v3:
time: 17.6 us; the launch traced here: 17.4 us
  Pallas kernels  16.7 us (95%)
  local copies, waits for them, and re-layouts  0.71 us (4%)
    pallas_call x1, Pallas kernels, shards_by_kernel(): pl.pallas_call(functools.partial(transform_kernel, lat_count), out_shape=...  16.7 us
    unnamed x1, local copies, waits for them, and re-layouts  0.71 us

profile of v3, /device:TPU:0, one launch (start us, length us, event | category | flops | bytes accessed | tf_op | source)
XLA Modules:
  0.0 17.4 jit_solution(17816913036124060002)
XLA Ops:
  0.0 16.7 %shard_map.37 = f32[8,32,160]{2,1,0:T(8,128)S(1)} custom-call(s32[64]{0:T(128)} %wave_hbm.1, s32[1,64]{1,0:T(1,128)} %bitcast.3, bf16[2,320,5120]{2,1,0:T(8,128)(2,1)} %field_ref.1, bf16[8,2,160,1280]{3,2,1,0:T(8,128)(2,1)} %legendre_ref.1), custom_call_target="tpu_custom_call" | custom-call | tf_op jit(solution)/shard_map/pallas_call | solution.py:553
  16.7 0.7 %copy.5 = f32[8,160,32]{1,2,0:T(8,128)} copy(f32[8,160,32]{1,2,0:T(8,128)S(1)} %bitcast.2) | data formatting | bytes 327680
